TPU v7x, 32 devices: a whole 2x2x4 slice. The times are simulated.
32 devices in a mesh: lon: 2 (over core), lat: 4 (over y, x), lead: 4 (over z).
Axes of the slice: x: 2, y: 2, z: 4, core: 2. Of those that a mesh axis runs over, the one named last changes fastest.
Arguments:
- activation: bfloat16 [16, 64, 4096], P('lead', 'lat', 'lon'), may hold values from -6 to 6
- pre_activation: bfloat16 [16, 64, 4096], P('lead', 'lat', 'lon'), may hold values from -8 to 8
- cotangent: bfloat16 [16, 64, 4096], P('lead', 'lat', 'lon'), may hold values from -6 to 6
- mode_weight: float32 [4608, 1024], P('lon'), may hold values from -1 to 1
- local_weight: float32 [32, 32], replicated, may hold values from -1 to 1
Outputs:
- input_grad: bfloat16 [16, 64, 4096], P('lead', 'lat', 'lon')
- mode_grad: float32 [4608, 1024], P('lon')
All inputs are finite; a program needn't handle non-finite values.
Results may differ from a plain program's by a relative error of at most 0.001.
Values sent between devices are 32-bit elements; how exact they have to be, the bound alone decides.
A program may use at most 64 MiB of HBM per device.

v0:
```python
import math

import jax
import jax.numpy as jnp
from jax import lax
from jax.sharding import PartitionSpec as P

MX = 24
MY = 24
MZ = 8
MODES = 4608


def make_basis(length, modes, start, count, stride):
    half = modes // 2
    order = jnp.arange(modes, dtype=jnp.int32)
    freq = jnp.where(order < half, order, order - half + 1)
    cells = start + stride * jnp.arange(count, dtype=jnp.int32)
    turns = freq[:, None] * cells[None, :] % length
    angle = 2.0 * math.pi / length * turns.astype(jnp.float32)
    waves = jnp.where(order[:, None] < half, jnp.cos(angle), jnp.sin(angle))
    weights = jnp.where(
        order == 0, jnp.float32(math.sqrt(1.0 / length)), jnp.float32(math.sqrt(2.0 / length))
    )
    return waves * weights[:, None]


def gelu_slope(value):
    normal_cdf = 0.5 * (1.0 + jax.scipy.special.erf(value / math.sqrt(2.0)))
    density = jnp.exp(-0.5 * value * value) / math.sqrt(2.0 * math.pi)
    return normal_cdf + value * density


def back_cells(coeffs, lon_basis, lat_basis, lead_basis):
    highest = lax.Precision.HIGHEST
    blocks = coeffs.reshape(
        lon_basis.shape[0], lat_basis.shape[0], lead_basis.shape[0], coeffs.shape[-1]
    )
    step = jnp.einsum("klqc,qz->zklc", blocks, lead_basis, precision=highest)
    step = jnp.einsum("zklc,ly->zykc", step, lat_basis, precision=highest)
    return jnp.einsum("zykc,kx->zyxc", step, lon_basis, precision=highest)


def on_device(activation, pre_activation, cotangent, mode_weight, local_weight):
    highest = lax.Precision.HIGHEST
    channels = local_weight.shape[0]
    lead_cells, lat_cells, merged = activation.shape
    lon_cells = merged // channels
    lon_count = lax.axis_size("lon")
    lon_total = lon_cells * lon_count
    lat_total = lat_cells * lax.axis_size("lat")
    lead_total = lead_cells * lax.axis_size("lead")
    lon_basis = make_basis(lon_total, MX, lax.axis_index("lon"), lon_cells, lon_count)
    lat_basis = make_basis(lat_total, MY, lax.axis_index("lat") * lat_cells, lat_cells, 1)
    lead_basis = make_basis(lead_total, MZ, lax.axis_index("lead") * lead_cells, lead_cells, 1)
    shape4 = (lead_cells, lat_cells, lon_cells, channels)
    grad_pre = cotangent.astype(jnp.float32).reshape(shape4) * gelu_slope(
        pre_activation.astype(jnp.float32).reshape(shape4)
    )
    stacked = jnp.concatenate([activation.astype(jnp.float32).reshape(shape4), grad_pre], axis=3)
    doubled = 2 * channels
    along_lon = jnp.einsum("zyxc,kx->zykc", stacked, lon_basis, precision=highest)
    along_lat = jnp.einsum("zykc,ly->zklc", along_lon, lat_basis, precision=highest)
    partial_sum = jnp.einsum("zklc,qz->klqc", along_lat, lead_basis, precision=highest).reshape(
        -1, doubled
    )
    summed = lax.psum(partial_sum, ("lat", "lead"))
    owned = lax.psum_scatter(summed, "lon", scatter_dimension=0, tiled=True)
    gain = math.sqrt(lon_total * lat_total * lead_total / MODES)
    coef = owned[:, :channels]
    spectral = gain * owned[:, channels:]
    owned_count = owned.shape[0]
    mode_grad = (coef[:, :, None] * spectral[:, None, :]).reshape(owned_count, channels * channels)
    mixing = mode_weight.reshape(owned_count, channels, channels)
    owned_adjoint = jnp.sum(mixing * spectral[:, None, :], axis=2)
    every_mode = lax.all_gather(owned_adjoint, "lon", axis=0, tiled=True)
    spread = back_cells(every_mode, lon_basis, lat_basis, lead_basis)
    local = jnp.einsum("zyxo,io->zyxi", grad_pre, local_weight, precision=highest)
    input_grad = (spread + local).reshape(lead_cells, lat_cells, merged)
    return (input_grad.astype(jnp.bfloat16), mode_grad)


def solution(mesh):
    in_specs = (
        P("lead", "lat", "lon"),
        P("lead", "lat", "lon"),
        P("lead", "lat", "lon"),
        P("lon", None),
        P(),
    )
    out_specs = (P("lead", "lat", "lon"), P("lon", None))
    return jax.shard_map(
        on_device, mesh=mesh, in_specs=in_specs, out_specs=out_specs, check_vma=False
    )
```

profile of v0, /device:TPU:0, one launch (start us, length us, event | category | flops | bytes accessed | tf_op | source)
XLA Modules:
  0.0 201.6 jit_solution(17013565351904019077)
XLA Ops:
  7.4 3.0 %reshape.99 = f32[4,16,64,32]{3,2,1,0:T(8,128)} reshape(bf16[4,16,2048]{2,1,0:T(8,128)(2,1)} %param.5) | data formatting | bytes 786432 | tf_op jit(solution)/shard_map/reshape | solution.py:60
  10.3 2.0 reshape.103
  12.4 2.0 reshape.101
  14.4 2.8 %fusion.4 = f32[4,16,64,32]{3,2,1,0:T(8,128)S(1)} fusion(f32[4,16,64,32]{3,2,1,0:T(8,128)} %reshape.101, f32[4,16,64,32]{3,2,1,0:T(8,128)} %reshape.103), kind=kLoop, calls=%fused_computation.7 | loop fusion | flops 1179648 | bytes 1572864 | tf_op jit(solution)/shard_map/mul | solution.py:57
  17.1 0.1 copy-done.1
  17.2 1.6 fusion.10
  18.8 1.3 convolution_bitcast_fusion
  20.1 4.7 %fusion.14 = f32[8,24,24,64]{3,0,2,1:T(8,128)} fusion(f32[4,24,24,64]{3,2,1,0:T(8,128)S(1)} %convolution_bitcast_fusion, f32[8]{0:T(128)S(1)} %compare_select_fusion, s32[4]{0:T(128)S(1)} %iota_add_fusion, s32[8]{0:T(128)S(1)} %add_select_fusion.3, pred[8]{0:T(512)(128)(4,1)S(1)} %iota_compare_fusion), kind=kOutput, calls=%fused_computation.19 | convolution fusion | flops 14156288 | bytes 1769560 | tf_op jit(solution)/shard_map/zklc,qz->klqc/dot_general | solution.py:64
  24.8 2.8 %copy.43 = f32[4608,64]{0,1:T(8,128)} copy(f32[4608,64]{1,0:T(8,128)} %bitcast.47) | data formatting | bytes 2359296 | tf_op jit(solution)/shard_map/reshape | solution.py:64
  27.6 0.2 all-reduce.2.cloned.1.call-start
  27.8 11.2 %reduce-scatter.2.cloned.1.call-done = f32[2304,64]{0,1:T(8,128)} async-done(((f32[4608,64]{0,1:T(8,128)}), f32[2304,64]{0,1:T(8,128)}) %reduce-scatter.2.cloned.1.call-update) | async-done | bytes 589840 | tf_op jit(solution)/shard_map/reduce_scatter | solution.py:68
  39.0 9.6 %copy.40 = f32[2304,1024]{0,1:T(8,128)} copy(f32[2304,1024]{1,0:T(8,128)} %param.8) | data formatting | bytes 18874368 | tf_op args[3]
  48.6 107.0 %all-reduce.2.cloned.1.call-done = f32[2304,64]{0,1:T(8,128)} async-done(((f32[2304,64]{0,1:T(8,128)}), f32[2304,64]{0,1:T(8,128)}) %all-reduce.2.cloned.1.call-update) | async-done | bytes 589840 | tf_op jit(solution)/shard_map/psum | solution.py:67
  155.6 1.1 fusion.60
  156.7 9.3 %broadcast_multiply_fusion = (f32[2304,32,32]{0,2,1:T(8,128)}, f32[2304,32]{0,1:T(8,128)S(1)}) fusion(f32[2304,32]{0,1:T(8,128)S(1)} %get-tuple-element.10, f32[2304,32]{0,1:T(8,128)S(1)} %get-tuple-element.11, f32[2304,1024]{0,1:T(8,128)} %copy.40), kind=kLoop, calls=%fused_computation.1 | loop fusion | flops 7004160 | bytes 19759104 | tf_op jit(solution)/shard_map/mul | solution.py:73
  166.1 9.6 %copy.49 = f32[2304,1024]{1,0:T(8,128)} copy(f32[2304,1024]{0,1:T(8,128)} %bitcast.45) | data formatting | bytes 18874368
  175.6 2.2 %all_gather.3 = f32[4608,32]{0,1:T(8,128)S(1)} all-gather(f32[2304,32]{0,1:T(8,128)S(1)} %get-tuple-element.13), channel_id=1, replica_groups=mesh['lon'=2,'lat'=4,'lead'=4] {'lon'}, dimensions={0}, use_global_device_ids=true | all-gather | bytes 884736 | tf_op jit(solution)/shard_map/all_gather | solution.py:76
  177.9 2.1 %copy.44 = f32[4608,32]{1,0:T(8,128)} copy(f32[4608,32]{0,1:T(8,128)S(1)} %all_gather.3) | data formatting | bytes 1179648 | tf_op jit(solution)/shard_map/all_gather | solution.py:76
  180.0 3.8 %fusion.32 = f32[4,24,24,32]{3,0,2,1:T(4,128)S(1)} fusion(f32[24,24,8,32]{3,2,1,0:T(8,128)} %bitcast.46, f32[8]{0:T(128)S(1)} %compare_select_fusion, s32[4]{0:T(128)S(1)} %iota_add_fusion, s32[8]{0:T(128)S(1)} %add_select_fusion.3, pred[8]{0:T(512)(128)(4,1)S(1)} %iota_compare_fusion), kind=kOutput, calls=%fused_computation.55 | convolution fusion | flops 7078400 | bytes 884824 | tf_op jit(solution)/shard_map/klqc,qz->zklc/dot_general | solution.py:39
  183.8 1.0 convolution_bitcast_fusion.2
  184.7 1.9 convolution_bitcast_fusion.1
  186.7 5.8 %fusion.9 = bf16[4,16,64,32]{2,3,1,0:T(8,128)(2,1)S(1)} fusion(f32[4,16,64,32]{2,3,1,0:T(8,128)S(1)} %convolution_bitcast_fusion.1, f32[4,16,64,32]{3,2,1,0:T(8,128)S(1)} %fusion.4, f32[32,32]{1,0:T(8,128)S(1)} %copy-done), kind=kOutput, calls=%fused_computation.15 | convolution fusion | flops 50593792 | bytes 1314816 | tf_op jit(solution)/shard_map/zyxo,io->zyxi/dot_general | solution.py:78
  192.5 0.5 copy.48
  193.0 1.8 convert_element_type.22
  (20 shorter events, 0.1 us)
Async XLA Ops:
  7.2 179.5 %copy-start = (f32[32,32]{1,0:T(8,128)S(1)}, f32[32,32]{1,0:T(8,128)}, u32[]{:S(2)}) copy-start(f32[32,32]{1,0:T(8,128)} %param.9) | copy-start | bytes 12292
  7.2 3.2 %copy-start.2 = (bf16[4,16,2048]{2,1,0:T(8,128)(2,1)S(1)}, bf16[4,16,2048]{2,1,0:T(8,128)(2,1)}, u32[]{:S(2)}) copy-start(bf16[4,16,2048]{2,1,0:T(8,128)(2,1)} %param.6) | copy-start | bytes 786436
  7.2 31.8 %reduce-scatter.2.cloned.1.call-start = ((), (), s32[]{:S(2)}) async-start(), calls=%async_computation.1 | async-start | bytes 1769472 | tf_op jit(solution)/shard_map/reduce_scatter | solution.py:68
  7.4 5.0 %copy-start.3 = (bf16[4,16,2048]{2,1,0:T(8,128)(2,1)S(1)}, bf16[4,16,2048]{2,1,0:T(8,128)(2,1)}, u32[]{:S(2)}) copy-start(bf16[4,16,2048]{2,1,0:T(8,128)(2,1)} %param.7) | copy-start | bytes 786436
  14.4 2.9 %copy-start.1 = (f32[4,16,64,32]{3,2,1,0:T(8,128)S(1)}, f32[4,16,64,32]{3,2,1,0:T(8,128)}, u32[]{:S(2)}) copy-start(f32[4,16,64,32]{3,2,1,0:T(8,128)} %reshape.99) | copy-start | bytes 1572868
  27.6 128.0 %all-reduce.2.cloned.1.call-start = ((), (), s32[]{:S(2)}) async-start(), calls=%async_computation.2 | async-start | bytes 1179648 | tf_op jit(solution)/shard_map/psum | solution.py:67
Sparse Core Ops, SparseCore 0:
  27.7 11.2 reduce-scatter.1
  44.3 111.2 all-reduce.1
where the time goes:
time: 202 us
  waiting for transfers between devices  118 us (58%)
  local copies, waits for them, and re-layouts  33.5 us (17%)
  matrix products  20 us (10%)
  between operations  14.2 us (7%)
  other arithmetic  13.2 us (7%)
  blocking collectives  2.22 us (1%)
    psum x1, waiting for transfers between devices, on_device(): summed = lax.psum(partial_sum, ('lat', 'lead'))  107 us
    unnamed x10, local copies, waits for them, and re-layouts  19.3 us
    reduce_scatter x1, waiting for transfers between devices, on_device(): owned = lax.psum_scatter(summed, 'lon', scatter_dimension=0, tiled=True)  11.2 us
    mul x1, other arithmetic, on_device(): coef[:, :, None] * spectral[:, None, :]  9.32 us
    dot_general x1, matrix products, on_device(): jnp.einsum('zyxo,io->zyxi', grad_pre, local_weight, precision=highest)  5.79 us
    dot_general x1, matrix products, on_device(): jnp.einsum('zklc,qz->klqc', along_lat, lead_basis, precision=highest)  4.7 us
  transfers between devices with their start and end apart: 2, of which 2 were waited for; matrix products, arithmetic and copies ran while one was open for 5% of the time, Pallas kernels for 0%

commit v1 on v0

--- a/solution.py
+++ b/solution.py
@@ -1,8 +1,13 @@
+import functools
 import math
 
 import jax
 import jax.numpy as jnp
+import ml_dtypes
+import numpy as np
 from jax import lax
+from jax.experimental import pallas as pl
+from jax.experimental.pallas import tpu as pltpu
 from jax.sharding import PartitionSpec as P
 
 MX = 24
@@ -80,6 +85,352 @@
     return (input_grad.astype(jnp.bfloat16), mode_grad)
 
 
+F32 = jnp.float32
+BF16 = jnp.bfloat16
+
+
+def host_basis(length, modes):
+    half = modes // 2
+    order = np.arange(modes)
+    freq = np.where(order < half, order, order - half + 1)
+    turns = (freq[:, None] * np.arange(length)[None, :]) % length
+    angle = 2.0 * np.pi / length * turns
+    waves = np.where(order[:, None] < half, np.cos(angle), np.sin(angle))
+    weights = np.where(order == 0, np.sqrt(1.0 / length), np.sqrt(2.0 / length))
+    return waves * weights[:, None]
+
+
+def halves(table):
+    table = np.asarray(table, np.float32)
+    high = table.astype(ml_dtypes.bfloat16)
+    low = (table - high.astype(np.float32)).astype(ml_dtypes.bfloat16)
+    return np.stack([high, low])
+
+
+def cut(value):
+    high = value.astype(BF16)
+    return high, (value - high.astype(F32)).astype(BF16)
+
+
+NN = (((1,), (0,)), ((), ()))
+NT = (((1,), (1,)), ((), ()))
+
+
+def mm(a, b, dims=NN):
+    return lax.dot_general(a, b, dims, preferred_element_type=F32)
+
+
+def mm3(table, b, dims=NN):
+    bh, bl = cut(b)
+    return mm(table[0], bh, dims) + mm(table[0], bl, dims) + mm(table[1], bh, dims)
+
+
+class Plan:
+    def __init__(self, mesh, arg_shape, channels):
+        self.nlon, self.nlat, self.nlead = (mesh.shape[n] for n in ("lon", "lat", "lead"))
+        nz, ny, merged = arg_shape
+        self.c = channels
+        self.zl, self.yl = nz // self.nlead, ny // self.nlat
+        self.nx = merged // channels
+        self.xl = self.nx // self.nlon
+        self.kp = MX // (self.nlon * self.nlat)
+        self.kc = self.kp * channels
+        self.lq = MY * MZ
+        self.zy = self.zl * self.yl
+        self.gain = math.sqrt(self.nx * ny * nz / MODES)
+        eye_z, eye_l = np.eye(self.zl), np.eye(MY)
+        bx, by, bz = host_basis(self.nx, MX), host_basis(ny, MY), host_basis(nz, MZ)
+        c = channels
+        lon_rows = np.stack(
+            [np.repeat(bx[:, d :: self.nlon], c, axis=1) for d in range(self.nlon)]
+        )
+        self.lon_table = halves(lon_rows)
+        self.same = np.tile(np.eye(c), (1, self.xl)).astype(ml_dtypes.bfloat16)
+        by_p = by.reshape(MY, self.nlat, self.yl)
+        bz_s = bz.reshape(MZ, self.nlead, self.zl)
+        eye_fz = np.eye(2 * self.zl)
+        self.lat_table = halves(
+            np.stack([np.kron(eye_fz, by_p[:, p]) for p in range(self.nlat)])
+        )
+        lead = np.einsum("qsz,lm->slqzm", bz_s, eye_l)
+        self.lead_table = halves(lead.reshape(self.nlead, self.lq, self.zl * MY))
+        self.lead_back = halves(
+            lead.transpose(0, 3, 4, 1, 2).reshape(self.nlead, self.zl * MY, self.lq)
+        )
+        back = np.einsum("lpy,zw->pzywl", by_p, eye_z)
+        self.lat_back = halves(back.reshape(self.nlat * self.zy, self.zl * MY))
+        cc = c * c
+        self.tile = np.concatenate(
+            [np.kron(np.eye(self.kp)[:, [k]], np.tile(np.eye(c), (1, 128 // c))) for k in range(self.kp)],
+            axis=1,
+        ).astype(ml_dtypes.bfloat16)
+        self.spread = np.stack(
+            [np.kron(np.eye(self.kp)[:, [k]], np.kron(np.eye(c), np.ones((1, c)))) for k in range(self.kp)]
+        ).astype(ml_dtypes.bfloat16)
+        self.gather = np.ascontiguousarray(self.spread.transpose(0, 2, 1))
+        wide = 256 // c
+        self.fan = np.tile(np.eye(c), (1, wide)).astype(np.float32)
+        self.block = np.kron(np.eye(wide), np.ones((c, c))).astype(np.float32)
+        self.cc = cc
+
+
+def remote_kernel(
+    plan, act, pre, cot, weight, lw, lon_t, same, lat_t, lead_t, lead_b, lat_b, tile, gather, fan, block,
+    modes_out, h_out, loc_out,
+    kx, xs, gbuf, sbuf, lonbuf, latsend, latrecv, leadbuf, wbuf, vbuf,
+    wsem, lon_s, lon_r, lat_s, lat_r, lead_s, lead_r, g_s, g_r, v_s, v_r, f_s, f_r,
+):
+    pn = plan
+    lon, lat, lead = (lax.axis_index(n) for n in ("lon", "lat", "lead"))
+    mesh_id = pl.DeviceIdType.MESH
+    other = 1 - lon
+    wcopy = pltpu.make_async_copy(
+        weight.at[pl.ds(pl.multiple_of(lat * (pn.kp * pn.lq), 8), pn.kp * pn.lq), :], wbuf, wsem
+    )
+    wcopy.start()
+    barrier = pltpu.get_barrier_semaphore()
+    pl.semaphore_signal(barrier, inc=1, device_id={"lon": other}, device_id_type=mesh_id)
+    for d in range(1, pn.nlat):
+        pl.semaphore_signal(
+            barrier, inc=1, device_id={"lat": lax.rem(lat + d, pn.nlat)}, device_id_type=mesh_id
+        )
+    for d in range(1, pn.nlead):
+        pl.semaphore_signal(
+            barrier, inc=1, device_id={"lead": lax.rem(lead + d, pn.nlead)}, device_id_type=mesh_id
+        )
+    c = pn.c
+    zy = pn.zy
+    mask = same[...]
+    for k in range(MX):
+        for h in range(2):
+            kx[h, k * c : (k + 1) * c, :] = lon_t[h, lon, k : k + 1, :] * mask
+
+    v = pre[...].astype(F32)
+    cdf = 0.5 * (1.0 + lax.erf(v * (1.0 / math.sqrt(2.0))))
+    density = jnp.exp(-0.5 * v * v) * (1.0 / math.sqrt(2.0 * math.pi))
+    grad = cot[...].astype(F32) * (cdf + v * density)
+    gh, gl = cut(grad)
+    xs[0:zy, :] = act[...]
+    xs[zy : 2 * zy, :] = gh
+    xs[2 * zy : 3 * zy, :] = jnp.zeros_like(gh)
+    xs[3 * zy : 4 * zy, :] = gl
+    half = MX // pn.nlon * c
+    for turn in range(2):
+        who = other if turn == 0 else lon
+        rows = pl.ds(pl.multiple_of(who * half, half), half)
+        p = mm(kx[0, rows, :], xs[...], NT)
+        q = mm(kx[1, rows, :], xs[0 : 2 * zy, :], NT)
+        sbuf[who] = p[:, 0 : 2 * zy] + p[:, 2 * zy :] + q
+        if turn == 0:
+            pl.semaphore_wait(barrier, 1 + (pn.nlat - 1) + (pn.nlead - 1))
+            lon_copy = pltpu.make_async_remote_copy(
+                src_ref=sbuf.at[other], dst_ref=lonbuf, send_sem=lon_s, recv_sem=lon_r,
+                device_id={"lon": other}, device_id_type=mesh_id,
+            )
+            lon_copy.start()
+    lon_copy.wait()
+    lat_copies = []
+    for d in list(range(1, pn.nlat)) + [0]:
+        p = lax.rem(lat + d, pn.nlat)
+        rows = pl.ds(pl.multiple_of(p * pn.kc, pn.kc), pn.kc)
+        value = sbuf[lon, rows, :] + lonbuf[rows, :]
+        if d == 0:
+            latrecv[lat] = value
+        else:
+            latsend[d - 1] = value
+            copy = pltpu.make_async_remote_copy(
+                src_ref=latsend.at[d - 1], dst_ref=latrecv.at[lat],
+                send_sem=lat_s.at[d - 1], recv_sem=lat_r.at[d - 1],
+                device_id={"lat": p}, device_id_type=mesh_id,
+            )
+            copy.start()
+            lat_copies.append(copy)
+    highest = lax.Precision.HIGHEST
+    left = lax.dot_general(fan[...], lw[...], (((0,), (1,)), ((), ())), precision=highest, preferred_element_type=F32)
+    both = jnp.dot(left, fan[...], precision=highest, preferred_element_type=F32) * block[...]
+    bh, bl = cut(both)
+    for t in range(pn.xl * c // 256):
+        cols = slice(t * 256, (t + 1) * 256)
+        hi, lo = xs[zy : 2 * zy, cols], xs[3 * zy : 4 * zy, cols]
+        loc_out[:, cols] = mm(hi, bh) + mm(lo, bh) + mm(hi, bl)
+    for copy in lat_copies:
+        copy.wait()
+    total = None
+    for p in range(pn.nlat):
+        term = mm3((lat_t[0, p], lat_t[1, p]), latrecv[p], NT)
+        total = term if total is None else total + term
+    leadbuf[lead] = total
+    lead_copies = []
+    for d in range(1, pn.nlead):
+        copy = pltpu.make_async_remote_copy(
+            src_ref=leadbuf.at[lead], dst_ref=leadbuf.at[lead],
+            send_sem=lead_s.at[d - 1], recv_sem=lead_r.at[d - 1],
+            device_id={"lead": lax.rem(lead + d, pn.nlead)}, device_id_type=mesh_id,
+        )
+        copy.start()
+        lead_copies.append(copy)
+    for copy in lead_copies:
+        copy.wait()
+    zm = pn.zl * MY
+    out = []
+    for f in range(2):
+        total = None
+        for s in range(pn.nlead):
+            term = mm3((lead_t[0, s], lead_t[1, s]), leadbuf[s, f * zm : (f + 1) * zm, :])
+            total = term if total is None else total + term
+        out.append(total)
+    coef, spectral = out[0], out[1] * pn.gain
+    modes_out[lat, 0] = coef
+    modes_out[lat, 1] = spectral
+    g_copies = []
+    for d in range(1, pn.nlat):
+        copy = pltpu.make_async_remote_copy(
+            src_ref=modes_out.at[lat], dst_ref=modes_out.at[lat],
+            send_sem=g_s.at[d - 1], recv_sem=g_r.at[d - 1],
+            device_id={"lat": lax.rem(lat + d, pn.nlat)}, device_id_type=mesh_id,
+        )
+        g_copies.append(copy)
+    wcopy.wait()
+    sh, sl = cut(spectral)
+    wide = mm(sh, tile[...]) + mm(sl, tile[...])
+    adjoint = None
+    for k in range(pn.kp):
+        four = wide[:, k * 128 : (k + 1) * 128]
+        prod = wbuf[k * pn.lq : (k + 1) * pn.lq, :] * jnp.concatenate([four] * (pn.cc // 128), axis=1)
+        ph, plow = cut(prod)
+        term = mm(ph, gather[k]) + mm(plow, gather[k])
+        adjoint = term if adjoint is None else adjoint + term
+    mine = mm3((lead_b[0, lead], lead_b[1, lead]), adjoint)
+    cells = mm3((lat_b[0], lat_b[1]), mine)
+    for p in range(pn.nlat):
+        vbuf[p] = cells[p * zy : (p + 1) * zy, :]
+    h_out[lon, lat] = vbuf[lat]
+    v_copies = []
+    for d in range(1, pn.nlat):
+        p = lax.rem(lat + d, pn.nlat)
+        copy = pltpu.make_async_remote_copy(
+            src_ref=vbuf.at[p], dst_ref=h_out.at[lon, lat],
+            send_sem=v_s.at[d - 1], recv_sem=v_r.at[d - 1],
+            device_id={"lat": p}, device_id_type=mesh_id,
+        )
+        copy.start()
+        v_copies.append(copy)
+    for copy in g_copies:
+        copy.start()
+    f_copies = []
+    for d in range(pn.nlat):
+        if d > 0:
+            v_copies[d - 1].wait_recv()
+        s = lax.rem(lat + pn.nlat - d, pn.nlat)
+        copy = pltpu.make_async_remote_copy(
+            src_ref=h_out.at[lon, s], dst_ref=h_out.at[lon, s],
+            send_sem=f_s.at[d], recv_sem=f_r.at[d],
+            device_id={"lon": other}, device_id_type=mesh_id,
+        )
+        copy.start()
+        f_copies.append(copy)
+    for copy in v_copies:
+        copy.wait_send()
+    for copy in f_copies:
+        copy.wait()
+    for copy in g_copies:
+        copy.wait()
+
+
+def finish_kernel(plan, modes, h_in, loc, lon_t, same, tile, spread, grad_out, mode_grad):
+    pn = plan
+    step = pl.program_id(0)
+    lon = lax.axis_index("lon")
+    c = pn.c
+    coef, spectral = modes[0, 0], modes[0, 1]
+    ch, cl = cut(coef)
+    sh, sl = cut(spectral)
+    r, t = spread[0], tile[...]
+    s4 = mm(sh, t) + mm(sl, t)
+    for j in range(pn.cc // 256):
+        cols = slice(j * 256, (j + 1) * 256)
+        big = mm(ch, r[:, cols]) + mm(cl, r[:, cols])
+        mode_grad[:, cols] = big * jnp.concatenate([s4, s4], axis=1)
+
+    @pl.when(step < pn.xl * c // 256)
+    def _():
+        cols = pl.ds(pl.multiple_of(step * 256, 256), 256)
+        mask = same[:, 0:256]
+        total = loc[:, cols]
+        for g in range(pn.nlon * pn.nlat):
+            parts = []
+            for h in range(2):
+                rows = [lon_t[h, lon, k : k + 1, cols] * mask for k in range(g * pn.kp, (g + 1) * pn.kp)]
+                parts.append(jnp.concatenate(rows, axis=0))
+            hh, hl = cut(h_in[g // pn.nlat, g % pn.nlat])
+            total += mm(hh, parts[0]) + mm(hl, parts[0]) + mm(hh, parts[1])
+        grad_out[:, cols] = total.astype(BF16)
+
+
+def fast_device(plan, activation, pre_activation, cotangent, mode_weight, local_weight):
+    pn = plan
+    merged = activation.shape[2]
+    flat = [v.reshape(pn.zy, merged) for v in (activation, pre_activation, cotangent)]
+    vm = pl.BlockSpec(memory_space=pltpu.VMEM)
+    hbm = pl.BlockSpec(memory_space=pl.ANY)
+    half = MX // pn.nlon * pn.c
+    dma = pltpu.SemaphoreType.DMA
+    modes, h, loc = pl.pallas_call(
+        functools.partial(remote_kernel, pn),
+        out_shape=(
+            jax.ShapeDtypeStruct((pn.nlat, 2, pn.lq, pn.kc), F32),
+            jax.ShapeDtypeStruct((pn.nlon, pn.nlat, pn.zy, pn.kc), F32),
+            jax.ShapeDtypeStruct((pn.zy, merged), F32),
+        ),
+        in_specs=[vm] * 3 + [hbm] + [vm] * 11,
+        out_specs=(vm,) * 3,
+        scratch_shapes=[
+            pltpu.VMEM((2, MX * pn.c, merged), BF16),
+            pltpu.VMEM((4 * pn.zy, merged), BF16),
+            pltpu.VMEM((8, 128), F32),
+            pltpu.VMEM((pn.nlon, half, 2 * pn.zy), F32),
+            pltpu.VMEM((half, 2 * pn.zy), F32),
+            pltpu.VMEM((pn.nlat - 1, pn.kc, 2 * pn.zy), F32),
+            pltpu.VMEM((pn.nlat, pn.kc, 2 * pn.zy), F32),
+            pltpu.VMEM((pn.nlead, 2 * pn.zl * MY, pn.kc), F32),
+            pltpu.VMEM((pn.kp * pn.lq, pn.cc), F32),
+            pltpu.VMEM((pn.nlat, pn.zy, pn.kc), F32),
+            dma, dma, dma,
+            dma((pn.nlat - 1,)), dma((pn.nlat - 1,)),
+            dma((pn.nlead - 1,)), dma((pn.nlead - 1,)),
+            dma((pn.nlat - 1,)), dma((pn.nlat - 1,)),
+            dma((pn.nlat - 1,)), dma((pn.nlat - 1,)),
+            dma((pn.nlat,)), dma((pn.nlat,)),
+        ],
+        compiler_params=pltpu.CompilerParams(
+            collective_id=0, has_side_effects=True, vmem_limit_bytes=56 * 2**20
+        ),
+        name="modes",
+    )(
+        *flat, mode_weight, local_weight, pn.lon_table, pn.same, pn.lat_table, pn.lead_table,
+        pn.lead_back, pn.lat_back, pn.tile, pn.gather, pn.fan, pn.block,
+    )
+    whole = lambda shape: pl.BlockSpec(shape, lambda i: (0,) * len(shape))
+    grad, mode_grad = pl.pallas_call(
+        functools.partial(finish_kernel, pn),
+        grid=(pn.nlat * pn.kp,),
+        out_shape=(
+            jax.ShapeDtypeStruct((pn.zy, merged), BF16),
+            jax.ShapeDtypeStruct((pn.nlat * pn.kp * pn.lq, pn.cc), F32),
+        ),
+        in_specs=[
+            pl.BlockSpec((1, 2, pn.lq, pn.kc), lambda i: (i // pn.kp, 0, 0, 0)),
+            whole(h.shape), whole(loc.shape), whole(pn.lon_table.shape), whole(pn.same.shape),
+            pl.BlockSpec((pn.kc, 128), lambda i: (0, i % pn.kp)),
+            pl.BlockSpec((1, pn.kc, pn.cc), lambda i: (i % pn.kp, 0, 0)),
+        ],
+        out_specs=(whole((pn.zy, merged)), pl.BlockSpec((pn.lq, pn.cc), lambda i: (i, 0))),
+        compiler_params=pltpu.CompilerParams(vmem_limit_bytes=40 * 2**20),
+        name="finish",
+    )(modes, h, loc, pn.lon_table, pn.same, pn.tile, pn.spread)
+    return grad.reshape(activation.shape), mode_grad
+
+
 def solution(mesh):
     in_specs = (
         P("lead", "lat", "lon"),
@@ -89,6 +440,21 @@
         P(),
     )
     out_specs = (P("lead", "lat", "lon"), P("lon", None))
-    return jax.shard_map(
-        on_device, mesh=mesh, in_specs=in_specs, out_specs=out_specs, check_vma=False
-    )
+
+    def whole(*args):
+        shape = args[0].shape
+        channels = args[4].shape[0]
+        body = on_device
+        if (
+            mesh.shape["lon"] == 2
+            and MX % (mesh.shape["lon"] * mesh.shape["lat"]) == 0
+            and MX * MY * MZ == args[3].shape[0]
+            and shape[2] // mesh.shape["lon"] % 256 == 0
+            and 128 % channels == 0
+        ):
+            body = functools.partial(fast_device, Plan(mesh, shape, channels))
+        return jax.shard_map(
+            body, mesh=mesh, in_specs=in_specs, out_specs=out_specs, check_vma=False
+        )(*args)
+
+    return whole

time: 202 us -> 50.2 us (0.25)
  waiting for transfers between devices: 118 us -> 0 us
  Pallas kernels: 0 us -> 45.7 us
  local copies, waits for them, and re-layouts: 33.5 us -> 3.14 us
  matrix products: 20 us -> 0 us
  between operations: 14.2 us -> 0.71 us
  other arithmetic: 13.2 us -> 0 us
  blocking collectives: 2.22 us -> 0 us
    psum x1 -> x0, waiting for transfers between devices: 107 us -> none  [on_device(): summed = lax.psum(partial_sum, ('lat', 'lead'))]
    pallas_call x0 -> x2, Pallas kernels: none -> 45.7 us  [the longest x1 35.8 us: fast_device(): pl.pallas_call(functools.partial(remote_kernel, pn), out_shape=(jax.Shape...]
    dot_general x7 -> x0, matrix products: 20 us -> none  [the longest x1 5.79 us: on_device(): jnp.einsum('zyxo,io->zyxi', grad_pre, local_weight, precision=highest)]
    unnamed x10 -> x14, local copies, waits for them, and re-layouts: 19.3 us -> 3.14 us
    mul x2 -> x0, other arithmetic: 12.1 us -> none  [the longest x1 9.32 us: on_device(): coef[:, :, None] * spectral[:, None, :]]
    reduce_scatter x1 -> x0, waiting for transfers between devices: 11.2 us -> none  [on_device(): owned = lax.psum_scatter(summed, 'lon', scatter_dimension=0, tiled=True)]
    reshape x4 -> x0, local copies, waits for them, and re-layouts: 9.79 us -> none  [the longest x1 2.96 us: on_device(): activation.astype(jnp.float32).reshape(shape4)]
    convert_element_type x2 -> x0, local copies, waits for them, and re-layouts: 2.3 us -> none  [on_device(): return (input_grad.astype(jnp.bfloat16), mode_grad)]
  transfers between devices with their start and end apart: 2 -> 0, of which waited for: 2 -> 0; matrix products, arithmetic and copies ran while one was open for 5% -> 0% of each run, Pallas kernels for 0% -> 0%
where the time goes in v1:
time: 50.2 us; the launch traced here: 49.6 us
  Pallas kernels  45.7 us (91%)
  local copies, waits for them, and re-layouts  3.14 us (6%)
  between operations  0.71 us (1%)
    pallas_call x1, Pallas kernels, fast_device(): pl.pallas_call(functools.partial(remote_kernel, pn), out_shape=(jax.Shape...  35.8 us
    pallas_call x1, Pallas kernels, fast_device(): pl.pallas_call(functools.partial(finish_kernel, pn), grid=(pn.nlat * pn.k...  9.93 us
    unnamed x14, local copies, waits for them, and re-layouts  3.14 us

profile of v1, /device:TPU:0, one launch (start us, length us, event | category | flops | bytes accessed | tf_op | source)
XLA Modules:
  0.0 49.6 jit_solution(5620498114916948655)
XLA Ops:
  0.6 0.0 copy-start.5
  0.6 0.0 copy-start.3
  0.7 0.0 copy-start
  0.7 0.0 copy-start.2
  0.7 35.8 %modes.1 = (f32[4,2,192,96]{3,2,1,0:T(8,128)}, f32[2,4,64,96]{3,2,1,0:T(8,128)}, f32[64,2048]{1,0:T(8,128)}) custom-call(bf16[64,2048]{1,0:T(8,128)(2,1)} %bitcast.4, bf16[64,2048]{1,0:T(8,128)(2,1)} %bitcast.5, bf16[64,2048]{1,0:T(8,128)(2,1)} %bitcast.6, f32[2304,1024]{1,0:T(8,128)} %weight.1, f32[32,32]{1,0:T(8,128)} %lw.1, ...), custom_call_target="tpu_custom_call" | custom-call | tf_op jit(solution)/shard_map/modes/pallas_call | solution.py:378
  36.5 0.0 copy-done.5
  36.5 0.0 copy-done.3
  36.5 0.0 copy-done
  36.5 0.0 copy-done.2
  36.5 0.0 copy-start.1
  36.5 1.1 %copy-done.1 = f32[4,2,192,96]{3,2,1,0:T(8,128)S(1)} copy-done((f32[4,2,192,96]{3,2,1,0:T(8,128)S(1)}, f32[4,2,192,96]{3,2,1,0:T(8,128)}, u32[]{:S(2)}) %copy-start.1) | copy-done | bytes 589848
  37.7 0.0 copy-start.4
  37.7 1.0 %copy-done.4 = f32[64,2048]{1,0:T(8,128)S(1)} copy-done((f32[64,2048]{1,0:T(8,128)S(1)}, f32[64,2048]{1,0:T(8,128)}, u32[]{:S(2)}) %copy-start.4) | copy-done | bytes 524312
  38.7 0.0 copy-start.6
  38.7 0.9 %copy-done.6 = f32[2,4,64,96]{3,2,1,0:T(8,128)S(1)} copy-done((f32[2,4,64,96]{3,2,1,0:T(8,128)S(1)}, f32[2,4,64,96]{3,2,1,0:T(8,128)}, u32[]{:S(2)}) %copy-start.6) | copy-done | bytes 196632
  39.7 9.9 %finish.1 = (bf16[64,2048]{1,0:T(8,128)(2,1)}, f32[2304,1024]{1,0:T(8,128)}) custom-call(f32[4,2,192,96]{3,2,1,0:T(8,128)S(1)} %copy-done.1, f32[2,4,64,96]{3,2,1,0:T(8,128)S(1)} %copy-done.6, f32[64,2048]{1,0:T(8,128)S(1)} %copy-done.4, bf16[2,2,24,2048]{3,2,1,0:T(8,128)(2,1)S(1)} %copy-done, bf16[32,2048]{1,0:T(8,128)(2,1)S(1)} %copy-done.3, ...), custom_call_target="tpu_custom_call" | custom-call | tf_op jit(solution)/shard_map/finish/pallas_call | solution.py:414
Async XLA Ops:
  0.6 35.9 %copy-start.5 = (bf16[96,384]{1,0:T(8,128)(2,1)S(1)}, bf16[96,384]{1,0:T(8,128)(2,1)}, u32[]{:S(2)}) copy-start(bf16[96,384]{1,0:T(8,128)(2,1)} %constant.28.clone.tile) | copy-start | bytes 221188
  0.6 35.9 %copy-start.3 = (bf16[32,2048]{1,0:T(8,128)(2,1)S(1)}, bf16[32,2048]{1,0:T(8,128)(2,1)}, u32[]{:S(2)}) copy-start(bf16[32,2048]{1,0:T(8,128)(2,1)} %constant.23.clone.same) | copy-start | bytes 393220
  0.7 35.9 %copy-start = (bf16[2,2,24,2048]{3,2,1,0:T(8,128)(2,1)S(1)}, bf16[2,2,24,2048]{3,2,1,0:T(8,128)(2,1)}, u32[]{:S(2)}) copy-start(bf16[2,2,24,2048]{3,2,1,0:T(8,128)(2,1)} %constant.22.clone.lon_t) | copy-start | bytes 1179652
  0.7 35.9 %copy-start.2 = (bf16[3,96,1024]{2,1,0:T(8,128)(2,1)S(1)}, bf16[3,96,1024]{2,1,0:T(8,128)(2,1)}, u32[]{:S(2)}) copy-start(bf16[3,96,1024]{2,1,0:T(8,128)(2,1)} %constant.32.clone.spread) | copy-start | bytes 1769476
  36.5 1.1 %copy-start.1 = (f32[4,2,192,96]{3,2,1,0:T(8,128)S(1)}, f32[4,2,192,96]{3,2,1,0:T(8,128)}, u32[]{:S(2)}) copy-start(f32[4,2,192,96]{3,2,1,0:T(8,128)} %get-tuple-element.7.modes) | copy-start | bytes 1769476
  37.7 1.0 %copy-start.4 = (f32[64,2048]{1,0:T(8,128)S(1)}, f32[64,2048]{1,0:T(8,128)}, u32[]{:S(2)}) copy-start(f32[64,2048]{1,0:T(8,128)} %get-tuple-element.9.loc) | copy-start | bytes 1572868
  38.7 0.9 %copy-start.6 = (f32[2,4,64,96]{3,2,1,0:T(8,128)S(1)}, f32[2,4,64,96]{3,2,1,0:T(8,128)}, u32[]{:S(2)}) copy-start(f32[2,4,64,96]{3,2,1,0:T(8,128)} %get-tuple-element.8.h_in) | copy-start | bytes 589828

commit v2 on v1

--- a/solution.py
+++ b/solution.py
@@ -177,7 +177,7 @@
 def remote_kernel(
     plan, act, pre, cot, weight, lw, lon_t, same, lat_t, lead_t, lead_b, lat_b, tile, gather, fan, block,
     modes_out, h_out, loc_out,
-    kx, xs, gbuf, sbuf, lonbuf, latsend, latrecv, leadbuf, wbuf, vbuf,
+    kx, xs, sbuf, lonbuf, latsend, latrecv, leadbuf, wbuf, vbuf,
     wsem, lon_s, lon_r, lat_s, lat_r, lead_s, lead_r, g_s, g_r, v_s, v_r, f_s, f_r,
 ):
     pn = plan
@@ -259,37 +259,41 @@
     for p in range(pn.nlat):
         term = mm3((lat_t[0, p], lat_t[1, p]), latrecv[p], NT)
         total = term if total is None else total + term
-    leadbuf[lead] = total
-    lead_copies = []
-    for d in range(1, pn.nlead):
-        copy = pltpu.make_async_remote_copy(
-            src_ref=leadbuf.at[lead], dst_ref=leadbuf.at[lead],
-            send_sem=lead_s.at[d - 1], recv_sem=lead_r.at[d - 1],
-            device_id={"lead": lax.rem(lead + d, pn.nlead)}, device_id_type=mesh_id,
-        )
-        copy.start()
-        lead_copies.append(copy)
-    for copy in lead_copies:
-        copy.wait()
     zm = pn.zl * MY
-    out = []
-    for f in range(2):
+    lead_copies = {}
+    for f in (1, 0):
+        leadbuf[lead, f] = total[f * zm : (f + 1) * zm, :]
+        for d in range(1, pn.nlead):
+            copy = pltpu.make_async_remote_copy(
+                src_ref=leadbuf.at[lead, f], dst_ref=leadbuf.at[lead, f],
+                send_sem=lead_s.at[f, d - 1], recv_sem=lead_r.at[f, d - 1],
+                device_id={"lead": lax.rem(lead + d, pn.nlead)}, device_id_type=mesh_id,
+            )
+            copy.start()
+            lead_copies[f, d] = copy
+    g_copies = []
+
+    def finish_lead(f):
+        for d in range(1, pn.nlead):
+            lead_copies[f, d].wait()
         total = None
         for s in range(pn.nlead):
-            term = mm3((lead_t[0, s], lead_t[1, s]), leadbuf[s, f * zm : (f + 1) * zm, :])
+            term = mm3((lead_t[0, s], lead_t[1, s]), leadbuf[s, f])
             total = term if total is None else total + term
-        out.append(total)
-    coef, spectral = out[0], out[1] * pn.gain
-    modes_out[lat, 0] = coef
-    modes_out[lat, 1] = spectral
-    g_copies = []
-    for d in range(1, pn.nlat):
-        copy = pltpu.make_async_remote_copy(
-            src_ref=modes_out.at[lat], dst_ref=modes_out.at[lat],
-            send_sem=g_s.at[d - 1], recv_sem=g_r.at[d - 1],
-            device_id={"lat": lax.rem(lat + d, pn.nlat)}, device_id_type=mesh_id,
-        )
-        g_copies.append(copy)
+        if f == 1:
+            total = total * pn.gain
+        modes_out[lat, f] = total
+        for d in range(1, pn.nlat):
+            copy = pltpu.make_async_remote_copy(
+                src_ref=modes_out.at[lat, f], dst_ref=modes_out.at[lat, f],
+                send_sem=g_s.at[f, d - 1], recv_sem=g_r.at[f, d - 1],
+                device_id={"lat": lax.rem(lat + d, pn.nlat)}, device_id_type=mesh_id,
+            )
+            copy.start()
+            g_copies.append(copy)
+        return total
+
+    spectral = finish_lead(1)
     wcopy.wait()
     sh, sl = cut(spectral)
     wide = mm(sh, tile[...]) + mm(sl, tile[...])
@@ -315,8 +319,7 @@
         )
         copy.start()
         v_copies.append(copy)
-    for copy in g_copies:
-        copy.start()
+    finish_lead(0)
     f_copies = []
     for d in range(pn.nlat):
         if d > 0:
@@ -337,34 +340,42 @@
         copy.wait()
 
 
-def finish_kernel(plan, modes, h_in, loc, lon_t, same, tile, spread, grad_out, mode_grad):
+def finish_kernel(plan, modes, h_in, loc, lon_t, same, tile, spread, grad_out, mode_grad, buf, sem):
     pn = plan
-    step = pl.program_id(0)
     lon = lax.axis_index("lon")
     c = pn.c
-    coef, spectral = modes[0, 0], modes[0, 1]
-    ch, cl = cut(coef)
-    sh, sl = cut(spectral)
-    r, t = spread[0], tile[...]
-    s4 = mm(sh, t) + mm(sl, t)
-    for j in range(pn.cc // 256):
-        cols = slice(j * 256, (j + 1) * 256)
-        big = mm(ch, r[:, cols]) + mm(cl, r[:, cols])
-        mode_grad[:, cols] = big * jnp.concatenate([s4, s4], axis=1)
-
-    @pl.when(step < pn.xl * c // 256)
-    def _():
-        cols = pl.ds(pl.multiple_of(step * 256, 256), 256)
-        mask = same[:, 0:256]
+    copies = []
+    for p in range(pn.nlat):
+        ch, cl = cut(modes[p, 0])
+        sh, sl = cut(modes[p, 1])
+        s4 = mm(sh, tile[...]) + mm(sl, tile[...])
+        for k in range(pn.kp):
+            chunk = p * pn.kp + k
+            rows = slice(chunk * pn.lq, (chunk + 1) * pn.lq)
+            four = s4[:, k * 128 : (k + 1) * 128]
+            two = jnp.concatenate([four, four], axis=1)
+            for j in range(pn.cc // 256):
+                cols = slice(j * 256, (j + 1) * 256)
+                big = mm(ch, spread[k, :, cols]) + mm(cl, spread[k, :, cols])
+                buf[rows, cols] = big * two
+            copy = pltpu.make_async_copy(buf.at[rows, :], mode_grad.at[rows, :], sem.at[chunk])
+            copy.start()
+            copies.append(copy)
+    mask = same[:, 0:256]
+    split = [[cut(h_in[a, b]) for b in range(pn.nlat)] for a in range(pn.nlon)]
+    for step in range(pn.xl * c // 256):
+        cols = slice(step * 256, (step + 1) * 256)
         total = loc[:, cols]
         for g in range(pn.nlon * pn.nlat):
             parts = []
             for h in range(2):
                 rows = [lon_t[h, lon, k : k + 1, cols] * mask for k in range(g * pn.kp, (g + 1) * pn.kp)]
                 parts.append(jnp.concatenate(rows, axis=0))
-            hh, hl = cut(h_in[g // pn.nlat, g % pn.nlat])
+            hh, hl = split[g // pn.nlat][g % pn.nlat]
             total += mm(hh, parts[0]) + mm(hl, parts[0]) + mm(hh, parts[1])
         grad_out[:, cols] = total.astype(BF16)
+    for copy in copies:
+        copy.wait()
 
 
 def fast_device(plan, activation, pre_activation, cotangent, mode_weight, local_weight):
@@ -378,27 +389,26 @@
     modes, h, loc = pl.pallas_call(
         functools.partial(remote_kernel, pn),
         out_shape=(
-            jax.ShapeDtypeStruct((pn.nlat, 2, pn.lq, pn.kc), F32),
-            jax.ShapeDtypeStruct((pn.nlon, pn.nlat, pn.zy, pn.kc), F32),
-            jax.ShapeDtypeStruct((pn.zy, merged), F32),
+            pltpu.VMEM((pn.nlat, 2, pn.lq, pn.kc), F32),
+            pltpu.VMEM((pn.nlon, pn.nlat, pn.zy, pn.kc), F32),
+            pltpu.VMEM((pn.zy, merged), F32),
         ),
         in_specs=[vm] * 3 + [hbm] + [vm] * 11,
         out_specs=(vm,) * 3,
         scratch_shapes=[
             pltpu.VMEM((2, MX * pn.c, merged), BF16),
             pltpu.VMEM((4 * pn.zy, merged), BF16),
-            pltpu.VMEM((8, 128), F32),
             pltpu.VMEM((pn.nlon, half, 2 * pn.zy), F32),
             pltpu.VMEM((half, 2 * pn.zy), F32),
             pltpu.VMEM((pn.nlat - 1, pn.kc, 2 * pn.zy), F32),
             pltpu.VMEM((pn.nlat, pn.kc, 2 * pn.zy), F32),
-            pltpu.VMEM((pn.nlead, 2 * pn.zl * MY, pn.kc), F32),
+            pltpu.VMEM((pn.nlead, 2, pn.zl * MY, pn.kc), F32),
             pltpu.VMEM((pn.kp * pn.lq, pn.cc), F32),
             pltpu.VMEM((pn.nlat, pn.zy, pn.kc), F32),
             dma, dma, dma,
             dma((pn.nlat - 1,)), dma((pn.nlat - 1,)),
-            dma((pn.nlead - 1,)), dma((pn.nlead - 1,)),
-            dma((pn.nlat - 1,)), dma((pn.nlat - 1,)),
+            dma((2, pn.nlead - 1)), dma((2, pn.nlead - 1)),
+            dma((2, pn.nlat - 1)), dma((2, pn.nlat - 1)),
             dma((pn.nlat - 1,)), dma((pn.nlat - 1,)),
             dma((pn.nlat,)), dma((pn.nlat,)),
         ],
@@ -410,21 +420,18 @@
         *flat, mode_weight, local_weight, pn.lon_table, pn.same, pn.lat_table, pn.lead_table,
         pn.lead_back, pn.lat_back, pn.tile, pn.gather, pn.fan, pn.block,
     )
-    whole = lambda shape: pl.BlockSpec(shape, lambda i: (0,) * len(shape))
     grad, mode_grad = pl.pallas_call(
         functools.partial(finish_kernel, pn),
-        grid=(pn.nlat * pn.kp,),
         out_shape=(
             jax.ShapeDtypeStruct((pn.zy, merged), BF16),
             jax.ShapeDtypeStruct((pn.nlat * pn.kp * pn.lq, pn.cc), F32),
         ),
-        in_specs=[
-            pl.BlockSpec((1, 2, pn.lq, pn.kc), lambda i: (i // pn.kp, 0, 0, 0)),
-            whole(h.shape), whole(loc.shape), whole(pn.lon_table.shape), whole(pn.same.shape),
-            pl.BlockSpec((pn.kc, 128), lambda i: (0, i % pn.kp)),
-            pl.BlockSpec((1, pn.kc, pn.cc), lambda i: (i % pn.kp, 0, 0)),
+        in_specs=[vm] * 7,
+        out_specs=(vm, hbm),
+        scratch_shapes=[
+            pltpu.VMEM((pn.nlat * pn.kp * pn.lq, pn.cc), F32),
+            dma((pn.nlat * pn.kp,)),
         ],
-        out_specs=(whole((pn.zy, merged)), pl.BlockSpec((pn.lq, pn.cc), lambda i: (i, 0))),
         compiler_params=pltpu.CompilerParams(vmem_limit_bytes=40 * 2**20),
         name="finish",
     )(modes, h, loc, pn.lon_table, pn.same, pn.tile, pn.spread)

time: 50.2 us -> 38 us (0.76)
  Pallas kernels: 45.7 us -> 37.2 us
  local copies, waits for them, and re-layouts: 3.14 us -> 0.03 us
    pallas_call x2, Pallas kernels: 45.7 us -> 37.2 us  [the longest x1 31.1 us: fast_device(): pl.pallas_call(functools.partial(remote_kernel, pn), out_shape=(pltpu.VME...]
    unnamed x14 -> x8, local copies, waits for them, and re-layouts: 3.14 us -> 0.03 us
where the time goes in v2:
time: 38 us; the launch traced here: 37.9 us
  Pallas kernels  37.2 us (98%)
  between operations  0.7 us (2%)
    pallas_call x1, Pallas kernels, fast_device(): pl.pallas_call(functools.partial(remote_kernel, pn), out_shape=(pltpu.VME...  31.1 us
    pallas_call x1, Pallas kernels, fast_device(): pl.pallas_call(functools.partial(finish_kernel, pn), out_shape=(jax.Shape...  6.04 us

profile of v2, /device:TPU:0, one launch (start us, length us, event | category | flops | bytes accessed | tf_op | source)
XLA Modules:
  0.0 37.9 jit_solution(3445363133470462165)
XLA Ops:
  0.6 0.0 copy-start.3
  0.6 0.0 copy-start.2
  0.7 0.0 copy-start
  0.7 0.0 copy-start.1
  0.7 31.1 %modes.1 = (f32[4,2,192,96]{3,2,1,0:T(8,128)S(1)}, f32[2,4,64,96]{3,2,1,0:T(8,128)S(1)}, f32[64,2048]{1,0:T(8,128)S(1)}) custom-call(bf16[64,2048]{1,0:T(8,128)(2,1)} %bitcast.4, bf16[64,2048]{1,0:T(8,128)(2,1)} %bitcast.5, bf16[64,2048]{1,0:T(8,128)(2,1)} %bitcast.6, f32[2304,1024]{1,0:T(8,128)} %weight.1, f32[32,32]{1,0:T(8,128)} %lw.1, ...), custom_call_target="tpu_custom_call" | custom-call | tf_op jit(solution)/shard_map/modes/pallas_call | solution.py:389
  31.8 0.0 copy-done.3
  31.8 0.0 copy-done.2
  31.8 0.0 copy-done
  31.8 0.0 copy-done.1
  31.9 6.0 %finish.1 = (bf16[64,2048]{1,0:T(8,128)(2,1)}, f32[2304,1024]{1,0:T(8,128)}) custom-call(f32[4,2,192,96]{3,2,1,0:T(8,128)S(1)} %get-tuple-element.7.modes, f32[2,4,64,96]{3,2,1,0:T(8,128)S(1)} %get-tuple-element.8.h_in, f32[64,2048]{1,0:T(8,128)S(1)} %get-tuple-element.9.loc, bf16[2,2,24,2048]{3,2,1,0:T(8,128)(2,1)S(1)} %copy-done, ...), custom_call_target="tpu_custom_call" | custom-call | tf_op jit(solution)/shard_map/finish/pallas_call | solution.py:423
Async XLA Ops:
  0.6 31.2 %copy-start.3 = (bf16[96,384]{1,0:T(8,128)(2,1)S(1)}, bf16[96,384]{1,0:T(8,128)(2,1)}, u32[]{:S(2)}) copy-start(bf16[96,384]{1,0:T(8,128)(2,1)} %constant.28.clone.tile) | copy-start | bytes 221188
  0.6 31.2 %copy-start.2 = (bf16[32,2048]{1,0:T(8,128)(2,1)S(1)}, bf16[32,2048]{1,0:T(8,128)(2,1)}, u32[]{:S(2)}) copy-start(bf16[32,2048]{1,0:T(8,128)(2,1)} %constant.23.clone.same) | copy-start | bytes 393220
  0.7 31.2 %copy-start = (bf16[2,2,24,2048]{3,2,1,0:T(8,128)(2,1)S(1)}, bf16[2,2,24,2048]{3,2,1,0:T(8,128)(2,1)}, u32[]{:S(2)}) copy-start(bf16[2,2,24,2048]{3,2,1,0:T(8,128)(2,1)} %constant.22.clone.lon_t) | copy-start | bytes 1179652
  0.7 31.2 %copy-start.1 = (bf16[3,96,1024]{2,1,0:T(8,128)(2,1)S(1)}, bf16[3,96,1024]{2,1,0:T(8,128)(2,1)}, u32[]{:S(2)}) copy-start(bf16[3,96,1024]{2,1,0:T(8,128)(2,1)} %constant.32.clone.spread) | copy-start | bytes 1769476

commit v3 on v2

--- a/solution.py
+++ b/solution.py
@@ -123,6 +123,24 @@
 def mm3(table, b, dims=NN):
     bh, bl = cut(b)
     return mm(table[0], bh, dims) + mm(table[0], bl, dims) + mm(table[1], bh, dims)
+
+
+def placed(shape, axis, channels, base):
+    wide = lax.broadcasted_iota(jnp.int32, shape, axis) // channels
+    narrow = lax.broadcasted_iota(jnp.int32, shape, 1 - axis) - base
+    return jnp.where(wide == narrow, 1.0, 0.0).astype(BF16)
+
+
+def fold(value):
+    r, lanes = value.shape[0] // 4, value.shape[1] // 3
+    last = jnp.concatenate([value[3 * r :, g * lanes : (g + 1) * lanes] for g in range(3)], axis=0)
+    return jnp.concatenate([value[: 3 * r], last], axis=1)
+
+
+def unfold(value):
+    r, lanes = value.shape[0] // 3, value.shape[1] // 4
+    last = jnp.concatenate([value[g * r : (g + 1) * r, 3 * lanes :] for g in range(3)], axis=1)
+    return jnp.concatenate([value[:, : 3 * lanes], last], axis=0)
 
 
 class Plan:
@@ -160,14 +178,11 @@
         back = np.einsum("lpy,zw->pzywl", by_p, eye_z)
         self.lat_back = halves(back.reshape(self.nlat * self.zy, self.zl * MY))
         cc = c * c
+        groups = 128 // c
         self.tile = np.concatenate(
-            [np.kron(np.eye(self.kp)[:, [k]], np.tile(np.eye(c), (1, 128 // c))) for k in range(self.kp)],
+            [np.kron(np.eye(groups)[:, [k]], np.tile(np.eye(c), (1, groups))) for k in range(groups)],
             axis=1,
         ).astype(ml_dtypes.bfloat16)
-        self.spread = np.stack(
-            [np.kron(np.eye(self.kp)[:, [k]], np.kron(np.eye(c), np.ones((1, c)))) for k in range(self.kp)]
-        ).astype(ml_dtypes.bfloat16)
-        self.gather = np.ascontiguousarray(self.spread.transpose(0, 2, 1))
         wide = 256 // c
         self.fan = np.tile(np.eye(c), (1, wide)).astype(np.float32)
         self.block = np.kron(np.eye(wide), np.ones((c, c))).astype(np.float32)
@@ -175,7 +190,7 @@
 
 
 def remote_kernel(
-    plan, act, pre, cot, weight, lw, lon_t, same, lat_t, lead_t, lead_b, lat_b, tile, gather, fan, block,
+    plan, act, pre, cot, weight, lw, lon_t, same, lat_t, lead_t, lead_b, lat_b, tile, fan, block,
     modes_out, h_out, loc_out,
     kx, xs, sbuf, lonbuf, latsend, latrecv, leadbuf, wbuf, vbuf,
     wsem, lon_s, lon_r, lat_s, lat_r, lead_s, lead_r, g_s, g_r, v_s, v_r, f_s, f_r,
@@ -262,7 +277,7 @@
     zm = pn.zl * MY
     lead_copies = {}
     for f in (1, 0):
-        leadbuf[lead, f] = total[f * zm : (f + 1) * zm, :]
+        leadbuf[lead, f] = fold(total[f * zm : (f + 1) * zm, :])
         for d in range(1, pn.nlead):
             copy = pltpu.make_async_remote_copy(
                 src_ref=leadbuf.at[lead, f], dst_ref=leadbuf.at[lead, f],
@@ -278,11 +293,11 @@
             lead_copies[f, d].wait()
         total = None
         for s in range(pn.nlead):
-            term = mm3((lead_t[0, s], lead_t[1, s]), leadbuf[s, f])
+            term = mm3((lead_t[0, s], lead_t[1, s]), unfold(leadbuf[s, f]))
             total = term if total is None else total + term
         if f == 1:
             total = total * pn.gain
-        modes_out[lat, f] = total
+        modes_out[lat, f] = fold(total)
         for d in range(1, pn.nlat):
             copy = pltpu.make_async_remote_copy(
                 src_ref=modes_out.at[lat, f], dst_ref=modes_out.at[lat, f],
@@ -296,18 +311,20 @@
     spectral = finish_lead(1)
     wcopy.wait()
     sh, sl = cut(spectral)
-    wide = mm(sh, tile[...]) + mm(sl, tile[...])
+    pick = tile[0 : pn.kc, 0 : pn.kp * 128]
+    wide = mm(sh, pick) + mm(sl, pick)
     adjoint = None
     for k in range(pn.kp):
         four = wide[:, k * 128 : (k + 1) * 128]
         prod = wbuf[k * pn.lq : (k + 1) * pn.lq, :] * jnp.concatenate([four] * (pn.cc // 128), axis=1)
         ph, plow = cut(prod)
-        term = mm(ph, gather[k]) + mm(plow, gather[k])
+        pick = placed((pn.cc, pn.kc), 0, c, k * c)
+        term = mm(ph, pick) + mm(plow, pick)
         adjoint = term if adjoint is None else adjoint + term
     mine = mm3((lead_b[0, lead], lead_b[1, lead]), adjoint)
     cells = mm3((lat_b[0], lat_b[1]), mine)
     for p in range(pn.nlat):
-        vbuf[p] = cells[p * zy : (p + 1) * zy, :]
+        vbuf[p] = fold(cells[p * zy : (p + 1) * zy, :])
     h_out[lon, lat] = vbuf[lat]
     v_copies = []
     for d in range(1, pn.nlat):
@@ -340,29 +357,34 @@
         copy.wait()
 
 
-def finish_kernel(plan, modes, h_in, loc, lon_t, same, tile, spread, grad_out, mode_grad, buf, sem):
+def finish_kernel(plan, modes, h_in, loc, lon_t, same, tile, grad_out, mode_grad, buf, sem):
     pn = plan
     lon = lax.axis_index("lon")
     c = pn.c
     copies = []
+    spread = [placed((128, pn.cc), 1, c, k * c) for k in range(pn.kp + 1)]
+    quarter = pn.lq // 4
     for p in range(pn.nlat):
         ch, cl = cut(modes[p, 0])
         sh, sl = cut(modes[p, 1])
         s4 = mm(sh, tile[...]) + mm(sl, tile[...])
         for k in range(pn.kp):
             chunk = p * pn.kp + k
+            part = slice(k * quarter, (k + 1) * quarter)
+            whole = (slice(0, 3 * quarter), k, chunk * pn.lq)
+            for source, which, first in (whole, (part, pn.kp, chunk * pn.lq + 3 * quarter)):
+                four = s4[source, which * 128 : (which + 1) * 128]
+                two = jnp.concatenate([four, four], axis=1)
+                for j in range(pn.cc // 256):
+                    cols = slice(j * 256, (j + 1) * 256)
+                    big = mm(ch[source], spread[which][:, cols]) + mm(cl[source], spread[which][:, cols])
+                    buf[first : first + four.shape[0], cols] = big * two
             rows = slice(chunk * pn.lq, (chunk + 1) * pn.lq)
-            four = s4[:, k * 128 : (k + 1) * 128]
-            two = jnp.concatenate([four, four], axis=1)
-            for j in range(pn.cc // 256):
-                cols = slice(j * 256, (j + 1) * 256)
-                big = mm(ch, spread[k, :, cols]) + mm(cl, spread[k, :, cols])
-                buf[rows, cols] = big * two
             copy = pltpu.make_async_copy(buf.at[rows, :], mode_grad.at[rows, :], sem.at[chunk])
             copy.start()
             copies.append(copy)
     mask = same[:, 0:256]
-    split = [[cut(h_in[a, b]) for b in range(pn.nlat)] for a in range(pn.nlon)]
+    split = [[cut(unfold(h_in[a, b])) for b in range(pn.nlat)] for a in range(pn.nlon)]
     for step in range(pn.xl * c // 256):
         cols = slice(step * 256, (step + 1) * 256)
         total = loc[:, cols]
@@ -389,11 +411,11 @@
     modes, h, loc = pl.pallas_call(
         functools.partial(remote_kernel, pn),
         out_shape=(
-            pltpu.VMEM((pn.nlat, 2, pn.lq, pn.kc), F32),
-            pltpu.VMEM((pn.nlon, pn.nlat, pn.zy, pn.kc), F32),
+            pltpu.VMEM((pn.nlat, 2, pn.lq // 4 * 3, 128), F32),
+            pltpu.VMEM((pn.nlon, pn.nlat, pn.zy // 4 * 3, 128), F32),
             pltpu.VMEM((pn.zy, merged), F32),
         ),
-        in_specs=[vm] * 3 + [hbm] + [vm] * 11,
+        in_specs=[vm] * 3 + [hbm] + [vm] * 10,
         out_specs=(vm,) * 3,
         scratch_shapes=[
             pltpu.VMEM((2, MX * pn.c, merged), BF16),
@@ -402,9 +424,9 @@
             pltpu.VMEM((half, 2 * pn.zy), F32),
             pltpu.VMEM((pn.nlat - 1, pn.kc, 2 * pn.zy), F32),
             pltpu.VMEM((pn.nlat, pn.kc, 2 * pn.zy), F32),
-            pltpu.VMEM((pn.nlead, 2, pn.zl * MY, pn.kc), F32),
+            pltpu.VMEM((pn.nlead, 2, pn.zl * MY // 4 * 3, 128), F32),
             pltpu.VMEM((pn.kp * pn.lq, pn.cc), F32),
-            pltpu.VMEM((pn.nlat, pn.zy, pn.kc), F32),
+            pltpu.VMEM((pn.nlat, pn.zy // 4 * 3, 128), F32),
             dma, dma, dma,
             dma((pn.nlat - 1,)), dma((pn.nlat - 1,)),
             dma((2, pn.nlead - 1)), dma((2, pn.nlead - 1)),
@@ -418,7 +440,7 @@
         name="modes",
     )(
         *flat, mode_weight, local_weight, pn.lon_table, pn.same, pn.lat_table, pn.lead_table,
-        pn.lead_back, pn.lat_back, pn.tile, pn.gather, pn.fan, pn.block,
+        pn.lead_back, pn.lat_back, pn.tile, pn.fan, pn.block,
     )
     grad, mode_grad = pl.pallas_call(
         functools.partial(finish_kernel, pn),
@@ -426,7 +448,7 @@
             jax.ShapeDtypeStruct((pn.zy, merged), BF16),
             jax.ShapeDtypeStruct((pn.nlat * pn.kp * pn.lq, pn.cc), F32),
         ),
-        in_specs=[vm] * 7,
+        in_specs=[vm] * 6,
         out_specs=(vm, hbm),
         scratch_shapes=[
             pltpu.VMEM((pn.nlat * pn.kp * pn.lq, pn.cc), F32),
@@ -434,7 +456,7 @@
         ],
         compiler_params=pltpu.CompilerParams(vmem_limit_bytes=40 * 2**20),
         name="finish",
-    )(modes, h, loc, pn.lon_table, pn.same, pn.tile, pn.spread)
+    )(modes, h, loc, pn.lon_table, pn.same, pn.tile)
     return grad.reshape(activation.shape), mode_grad
 
 
@@ -457,7 +479,9 @@
             and MX % (mesh.shape["lon"] * mesh.shape["lat"]) == 0
             and MX * MY * MZ == args[3].shape[0]
             and shape[2] // mesh.shape["lon"] % 256 == 0
-            and 128 % channels == 0
+            and 4 * channels == 128
+            and MX * channels == 96 * mesh.shape["lon"] * mesh.shape["lat"]
+            and mesh.shape["lead"] * 4 == shape[0]
         ):
             body = functools.partial(fast_device, Plan(mesh, shape, channels))
         return jax.shard_map(

time: 38 us -> 34.7 us (0.913)
  Pallas kernels: 37.2 us -> 33.8 us
    pallas_call x1, Pallas kernels: 31.1 us -> 27.6 us  [fast_device(): pl.pallas_call(functools.partial(remote_kernel, pn), out_shape=(pltpu.VME...]
where the time goes in v3:
time: 34.7 us; the launch traced here: 34.5 us
  Pallas kernels  33.8 us (97%)
  between operations  0.69 us (2%)
    pallas_call x1, Pallas kernels, fast_device(): pl.pallas_call(functools.partial(remote_kernel, pn), out_shape=(pltpu.VME...  27.6 us
    pallas_call x1, Pallas kernels, fast_device(): pl.pallas_call(functools.partial(finish_kernel, pn), out_shape=(jax.Shape...  6.2 us

profile of v3, /device:TPU:0, one launch (start us, length us, event | category | flops | bytes accessed | tf_op | source)
XLA Modules:
  0.0 34.5 jit_solution(1490030482448433149)
XLA Ops:
  0.6 0.0 copy-start.1
  0.6 0.0 copy-start.2
  0.7 0.0 copy-start
  0.7 27.6 %modes.1 = (f32[4,2,144,128]{3,2,1,0:T(8,128)S(1)}, f32[2,4,48,128]{3,2,1,0:T(8,128)S(1)}, f32[64,2048]{1,0:T(8,128)S(1)}) custom-call(bf16[64,2048]{1,0:T(8,128)(2,1)} %bitcast.4, bf16[64,2048]{1,0:T(8,128)(2,1)} %bitcast.5, bf16[64,2048]{1,0:T(8,128)(2,1)} %bitcast.6, f32[2304,1024]{1,0:T(8,128)} %weight.1, f32[32,32]{1,0:T(8,128)} %lw.1, ...), custom_call_target="tpu_custom_call" | custom-call | tf_op jit(solution)/shard_map/modes/pallas_call | solution.py:411
  28.3 0.0 copy-done.1
  28.3 0.0 copy-done.2
  28.3 0.0 copy-done
  28.3 6.2 %finish.1 = (bf16[64,2048]{1,0:T(8,128)(2,1)}, f32[2304,1024]{1,0:T(8,128)}) custom-call(f32[4,2,144,128]{3,2,1,0:T(8,128)S(1)} %get-tuple-element.7.modes, f32[2,4,48,128]{3,2,1,0:T(8,128)S(1)} %get-tuple-element.8.h_in, f32[64,2048]{1,0:T(8,128)S(1)} %get-tuple-element.9.loc, bf16[2,2,24,2048]{3,2,1,0:T(8,128)(2,1)S(1)} %copy-done, ...), custom_call_target="tpu_custom_call" | custom-call | tf_op jit(solution)/shard_map/finish/pallas_call | solution.py:445
Async XLA Ops:
  0.6 27.7 %copy-start.1 = (bf16[128,512]{1,0:T(8,128)(2,1)S(1)}, bf16[128,512]{1,0:T(8,128)(2,1)}, u32[]{:S(2)}) copy-start(bf16[128,512]{1,0:T(8,128)(2,1)} %constant.24.clone.tile) | copy-start | bytes 393220
  0.6 27.7 %copy-start.2 = (bf16[32,2048]{1,0:T(8,128)(2,1)S(1)}, bf16[32,2048]{1,0:T(8,128)(2,1)}, u32[]{:S(2)}) copy-start(bf16[32,2048]{1,0:T(8,128)(2,1)} %constant.19.clone.same) | copy-start | bytes 393220
  0.7 27.7 %copy-start = (bf16[2,2,24,2048]{3,2,1,0:T(8,128)(2,1)S(1)}, bf16[2,2,24,2048]{3,2,1,0:T(8,128)(2,1)}, u32[]{:S(2)}) copy-start(bf16[2,2,24,2048]{3,2,1,0:T(8,128)(2,1)} %constant.18.clone.lon_t) | copy-start | bytes 1179652
